TPU v7x, 32 devices: a whole 2x2x4 slice. The times are simulated.
32 devices in a mesh: grp: 2 (over y), row: 4 (over z), col: 4 (over x, core).
Axes of the slice: x: 2, y: 2, z: 4, core: 2. Of those that a mesh axis runs over, the one named last changes fastest.
Arguments:
- factor: float32 [4, 1024, 1024], P('grp', ('row', 'col')), may hold values from -0.1875 to 0.1875
- pivots: float32 [4, 1024], P('grp', ('row', 'col')), may hold values from 0.5 to 2
- constraints: float32 [4, 1024, 4096], P('grp', None, ('col', 'row')), may hold values from -0.09375 to 0.09375
Outputs:
- q_panels: float32 [4, 1024, 4096], P('row', 'grp', 'col')
All inputs are finite; a program needn't handle non-finite values.
Results may differ from a plain program's by a relative error of at most 0.0011.
Values may be sent and summed in bfloat16 or wider, within the bound.
A program may use at most 64 MiB of HBM per device.

v0:
```python
import jax
import jax.numpy as jnp
from jax import lax
from jax.sharding import PartitionSpec as P

exact_mode = lax.Precision.HIGHEST


def body(factor, pivots, constraints):
    factor_piece = lax.all_gather(factor, ("row", "col"), axis=1, tiled=True)
    pivot_piece = lax.all_gather(pivots, ("row", "col"), axis=1, tiled=True)
    row_ids = lax.broadcasted_iota(jnp.int32, factor_piece.shape, 1)
    col_ids = lax.broadcasted_iota(jnp.int32, factor_piece.shape, 2)
    triangle = jnp.where(col_ids < row_ids, factor_piece, jnp.zeros_like(factor_piece))
    product = jnp.einsum(
        "brm,bms->brs",
        triangle,
        constraints,
        precision=exact_mode,
        preferred_element_type=jnp.float32,
    )
    scaled = pivot_piece[:, :, None] * constraints
    projected_full = product + scaled
    projected = projected_full.astype(jnp.bfloat16)
    column_panel = lax.all_gather(projected, "row", axis=2, tiled=True)
    gram_tile = lax.dot_general(
        lax.all_gather(projected, "col", axis=2, tiled=True),
        column_panel,
        (((0, 1), (0, 1)), ((), ())),
        preferred_element_type=jnp.float32,
    )
    summed = lax.psum_scatter(gram_tile, "grp", scatter_dimension=0, tiled=True)
    return summed[None]


def solution(mesh):
    in_specs = (
        P("grp", ("row", "col"), None),
        P("grp", ("row", "col")),
        P("grp", None, ("col", "row")),
    )
    out_specs = P("row", "grp", "col")
    return jax.shard_map(body, mesh=mesh, in_specs=in_specs, out_specs=out_specs, check_vma=False)
```

profile of v0, /device:TPU:0, one launch (start us, length us, event | category | flops | bytes accessed | tf_op | source)
XLA Modules:
  0.0 284.5 jit_solution(2137502294490413980)
XLA Ops:
  6.5 0.0 all-gather.5.cloned.1.call-start
  6.5 0.7 all-gather.5.cloned.1.call-update
  7.3 0.0 all-gather.7.cloned.1.call-start
  7.3 23.4 %all-gather = f32[16,64,2]{1,2,0:T(2,128)S(1)} all-gather(f32[1,64,2]{1,2,0:T(2,128)} %bitcast.13), channel_id=1, replica_groups=mesh['grp'=2,'row'=4,'col'=4] {'row','col'}, dimensions={0}, use_global_device_ids=true | all-gather | bytes 8704 | tf_op jit(solution)/shard_map/all_gather | solution.py:11
  30.8 0.1 reshape.2
  30.8 56.4 %all-gather.5.cloned.1.call-done = f32[2,1024,1024]{2,1,0:T(8,128)} async-done(((f32[2,64,1024]{2,1,0:T(8,128)}), f32[2,1024,1024]{2,1,0:T(8,128)}) %all-gather.5.cloned.1.call-update) | async-done | bytes 8388624 | tf_op jit(solution)/shard_map/all_gather | solution.py:10
  87.2 12.5 %add_convert_fusion = bf16[2,1024,256]{2,1,0:T(8,128)(2,1)} fusion(f32[2,1024,256]{2,1,0:T(8,128)} %param.5, f32[2,1024,1024]{2,1,0:T(8,128)} %all-gather.5.cloned.1.call-done, f32[2,1024]{1,0:T(2,128)S(1)} %bitcast.12), kind=kOutput, calls=%fused_computation.5 | convolution fusion | flops 6448218112 | bytes 11542528 | tf_op jit(solution)/shard_map/brm,bms->brs/dot_general | solution.py:15
  99.7 0.0 all-gather.7.cloned.1.call-update
  99.7 0.0 all-gather.9.cloned.1.call-start
  99.8 0.7 all-gather.9.cloned.1.call-update
  100.5 0.0 reduce-scatter.2.cloned.1.call-start
  100.5 32.6 %all-gather.7.cloned.1.call-done = bf16[2,1024,1024]{2,1,0:T(8,128)(2,1)} async-done(((bf16[2,1024,256]{2,1,0:T(8,128)(2,1)}), bf16[2,1024,1024]{2,1,0:T(8,128)(2,1)}) %all-gather.7.cloned.1.call-update) | async-done | bytes 4194320 | tf_op jit(solution)/shard_map/all_gather | solution.py:27
  133.1 82.2 %all-gather.9.cloned.1.call-done = bf16[2,1024,1024]{2,1,0:T(8,128)(2,1)} async-done(((bf16[2,1024,256]{2,1,0:T(8,128)(2,1)}), bf16[2,1024,1024]{2,1,0:T(8,128)(2,1)}) %all-gather.9.cloned.1.call-update) | async-done | bytes 4194320 | tf_op jit(solution)/shard_map/all_gather | solution.py:25
  215.3 10.0 %convolution_bitcast_fusion = f32[1024,1024]{1,0:T(8,128)} fusion(bf16[2,1024,1024]{2,1,0:T(8,128)(2,1)} %all-gather.7.cloned.1.call-done, bf16[2,1024,1024]{2,1,0:T(8,128)(2,1)} %all-gather.9.cloned.1.call-done), kind=kOutput, calls=%fused_computation.4 | convolution fusion | flops 4294967296 | bytes 12582912 | tf_op jit(solution)/shard_map/dot_general | solution.py:26
  225.3 0.0 reduce-scatter.2.cloned.1.call-update
  225.3 52.7 %reduce-scatter.2.cloned.1.call-done = f32[512,1024]{1,0:T(8,128)} async-done(((f32[1024,1024]{1,0:T(8,128)}), f32[512,1024]{1,0:T(8,128)}) %reduce-scatter.2.cloned.1.call-update) | async-done | bytes 2097168 | tf_op jit(solution)/shard_map/reduce_scatter | solution.py:32
  (1 shorter events, 0.0 us)
Async XLA Ops:
  6.5 80.7 %all-gather.5.cloned.1.call-start = ((), (), s32[]{:S(2)}) async-start(), calls=%async_computation.1 | async-start | bytes 8912896 | tf_op jit(solution)/shard_map/all_gather | solution.py:10
  7.3 125.9 %all-gather.7.cloned.1.call-start = ((), (), s32[]{:S(2)}) async-start(), calls=%async_computation.2 | async-start | bytes 5242880 | tf_op jit(solution)/shard_map/all_gather | solution.py:27
  99.7 115.6 %all-gather.9.cloned.1.call-start = ((), (), s32[]{:S(2)}) async-start(), calls=%async_computation.3 | async-start | bytes 5242880 | tf_op jit(solution)/shard_map/all_gather | solution.py:25
  100.5 177.5 %reduce-scatter.2.cloned.1.call-start = ((), (), s32[]{:S(2)}) async-start(), calls=%async_computation.4 | async-start | bytes 6291456 | tf_op jit(solution)/shard_map/reduce_scatter | solution.py:32
Sparse Core Ops, SparseCore 0:
  9.5 77.6 all-gather.4
  99.8 33.2 all-gather.6
  134.7 80.5 all-gather.8
  225.5 52.4 reduce-scatter.1
where the time goes:
time: 285 us
  waiting for transfers between devices  225 us (79%)
  blocking collectives  23.4 us (8%)
  matrix products  22.5 us (8%)
  between operations  13.1 us (5%)
    all_gather x1, waiting for transfers between devices, body(): column_panel = lax.all_gather(projected, 'row', axis=2, tiled=True)  82.2 us
    all_gather x1, waiting for transfers between devices, body(): factor_piece = lax.all_gather(factor, ('row', 'col'), axis=1, tiled=True)  56.4 us
    reduce_scatter x1, waiting for transfers between devices, body(): summed = lax.psum_scatter(gram_tile, 'grp', scatter_dimension=0, tiled=True)  52.7 us
    all_gather x1, waiting for transfers between devices, body(): lax.all_gather(projected, 'col', axis=2, tiled=True)  32.6 us
    all_gather x1, blocking collectives, body(): pivot_piece = lax.all_gather(pivots, ('row', 'col'), axis=1, tiled=True)  23.4 us
    dot_general x1, matrix products, body(): jnp.einsum('brm,bms->brs', triangle, constraints, precision=exact_mode, p...  12.5 us
    dot_general x1, matrix products, body(): lax.dot_general(lax.all_gather(projected, 'col', axis=2, tiled=True), col...  10 us
  transfers between devices with their start and end apart: 4, of which 4 were waited for; matrix products, arithmetic and copies ran while one was open for 0% of the time, Pallas kernels for 0%

commit v1 on v0

v1 whole, which is shorter than its diff:
```python
import functools
import jax
import jax.numpy as jnp
from jax import lax
from jax.experimental import pallas as pl
from jax.experimental.pallas import tpu as pltpu
from jax.sharding import PartitionSpec as P

MESH = pl.DeviceIdType.MESH
f32 = jnp.float32
bf16 = jnp.bfloat16
W = 256


def kernel(G, nb, tin, c_hbm, out, tbuf, cbuf, chi, clo, acc, colbuf, rowt, sbuf, rbuf,
           csem, tss, trs, pzs, pzr, pxs, pxr, rss, rsr):
    g, z, c = lax.axis_index("grp"), lax.axis_index("row"), lax.axis_index("col")
    sib = c + 1 - 2 * (c % 2)
    xn = (c + 2) % 4
    d_up, d_dn = (g, z + 1, c), (g, z - 1, c)
    d_xn, d_sib = (g, z, xn), (g, z, sib)
    d_y = (1 - g, z, c)
    piece = tin.shape[2]

    def order(zz, j):
        if j == 0:
            return zz
        if j == 1:
            return zz - 1 + 2 * ((3 - zz) // 3)
        if j == 2:
            return zz + 1 + (3 - zz) // 3 - 3 * (zz // 3)
        return 3 - 3 * (zz // 2)

    cload = pltpu.make_async_copy(c_hbm, cbuf, csem)
    cload.start()

    bar = pltpu.get_barrier_semaphore()

    def hello(dev):
        pl.semaphore_signal(bar, inc=1, device_id=dev, device_id_type=MESH)

    hello(d_xn)
    hello(d_sib)
    if G == 2:
        hello(d_y)

    @pl.when(z < 3)
    def _():
        hello(d_up)

    @pl.when(z > 0)
    def _():
        hello(d_dn)

    for kc in range(4):
        @pl.when(kc <= z)
        def _():
            tbuf[kc, :, pl.ds(pl.multiple_of(W * z + piece * c, piece), piece), :] = tin[kc]

    pl.semaphore_wait(bar, (3 if G == 2 else 2) + (z + 3) // 4 + 1 - z // 3)

    def remote(ref, ss, rs, dev):
        return pltpu.make_async_remote_copy(
            src_ref=ref, dst_ref=ref, send_sem=ss, recv_sem=rs, device_id=dev, device_id_type=MESH)

    def tcopy(route, arrive, r, kc, col, dev):
        ref = tbuf.at[kc, :, pl.ds(pl.multiple_of(W * r + piece * col, piece), piece), :]
        return remote(ref, tss.at[route, r, kc], trs.at[arrive, r, kc], dev)

    def t_up(r, kc):
        return tcopy(0, 0, r, kc, c, d_up)

    def t_dn(r, kc):
        return tcopy(1, 0, r, kc, c, d_dn)

    def t_xn(r, kc):
        return tcopy(2, 1, r, kc, c, d_xn)

    def t_sib(r, kc):
        return tcopy(3, 2, r, kc, c, d_sib)

    def t_fwd(r, kc):
        return tcopy(4, 3, r, kc, xn, d_sib)

    def t_first(j):
        r = order(z, j)

        @pl.loop(0, r + 1)
        def _(kc):
            if j > 0:
                t_up(r, kc).wait_recv()

            @pl.when((r <= z) & (z < 3))
            def _():
                t_up(r, kc).start()

            @pl.when((r >= z) & (z > 0))
            def _():
                t_dn(r, kc).start()

            t_xn(r, kc).start()
            t_sib(r, kc).start()

    def t_second(j):
        r = order(z, j)

        @pl.loop(0, r + 1)
        def _(kc):
            t_xn(r, kc).wait_recv()
            t_fwd(r, kc).start()

    def pz(s, rg, up):
        return remote(colbuf.at[s, rg], pzs.at[0 if up else 1, s, rg], pzr.at[s, rg], d_up if up else d_dn)

    def px(route, col, rg):
        return remote(rowt.at[col, rg], pxs.at[route, rg], pxr.at[route, rg], d_xn if route == 0 else d_sib)

    def project(j):
        r = order(z, j)

        @pl.loop(0, r + 1)
        def _(kc):
            t_sib(r, kc).wait_recv()
            t_fwd(r, kc).wait_recv()

        rows = pl.ds(pl.multiple_of(W * r, W), W)
        for b in range(nb):
            acc[...] = jnp.zeros_like(acc)

            @pl.loop(0, r + 1)
            def _(kc):
                t = tbuf[kc, b, rows, :]
                th = t.astype(bf16)
                tl = (t - th.astype(f32)).astype(bf16)
                ks = pl.ds(pl.multiple_of(W * kc, W), W)
                ch = chi[b, ks, :]
                acc[...] += (jnp.dot(th, ch, preferred_element_type=f32)
                             + jnp.dot(th, clo[b, ks, :], preferred_element_type=f32)
                             + jnp.dot(tl, ch, preferred_element_type=f32))

            full = acc[...]
            colbuf[z, r, W * b:W * (b + 1), :] = full.astype(bf16)
            rowt[c, r, :, W * b:W * (b + 1)] = full.T.astype(bf16)

        @pl.when(z < 3)
        def _():
            pz(z, r, True).start()

        @pl.when(z > 0)
        def _():
            pz(z, r, False).start()

        px(0, c, r).start()
        px(1, c, r).start()

    t_first(0)
    cload.wait()
    for b in range(nb):
        cc = cbuf[b]
        hi = cc.astype(bf16)
        chi[b] = hi
        clo[b] = (cc - hi.astype(f32)).astype(bf16)
    for j in range(1, 4):
        t_first(j)
        t_second(j - 1)
        project(j - 1)
    t_second(3)
    project(3)

    def block(cp, s):
        total = jnp.dot(rowt[cp, 0], colbuf[s, 0], preferred_element_type=f32)
        for rg in range(1, 4):
            total += jnp.dot(rowt[cp, rg], colbuf[s, rg], preferred_element_type=f32)
        return total

    def rs(s):
        return pltpu.make_async_remote_copy(
            src_ref=sbuf.at[s], dst_ref=rbuf.at[s], send_sem=rss.at[s], recv_sem=rsr.at[s],
            device_id=d_y, device_id_type=MESH)

    def gram(s):
        cols = pl.ds(pl.multiple_of(W * s, W), W)
        if G == 2:
            @pl.loop(0, 2)
            def _(i):
                sbuf[s, pl.ds(pl.multiple_of(W * i, W), W), :] = block(2 * (1 - g) + i, s)

            rs(s).start()

            @pl.loop(0, 2)
            def _(i):
                out[pl.ds(pl.multiple_of(W * i, W), W), cols] = block(2 * g + i, s)
        else:
            @pl.loop(0, 4)
            def _(i):
                out[pl.ds(pl.multiple_of(W * i, W), W), cols] = block(i, s)

    def z_arrivals(d, i):
        lo, hi = z - d, z + d

        @pl.when(lo >= 0)
        def _():
            rg = order(lo, i)
            pz(lo, rg, True).wait_recv()

            @pl.when(z < 3)
            def _():
                pz(lo, rg, True).start()

        @pl.when(hi <= 3)
        def _():
            rg = order(hi, i)
            pz(hi, rg, False).wait_recv()

            @pl.when(z > 0)
            def _():
                pz(hi, rg, False).start()

    for i in range(4):
        r = order(z, i)
        px(0, c, r).wait_recv()
        px(2, xn, r).start()
        z_arrivals(1, i)
    for i in range(4):
        px(1, c, i).wait_recv()
        px(2, c, i).wait_recv()
    gram(z)
    for d in (1, 2, 3):
        if d > 1:
            for i in range(4):
                z_arrivals(d, i)

        @pl.when(z - d >= 0)
        def _():
            gram(z - d)

        @pl.when(z + d <= 3)
        def _():
            gram(z + d)

    if G == 2:
        def finish(s):
            cols = pl.ds(pl.multiple_of(W * s, W), W)
            rs(s).wait_recv()
            out[:, cols] = out[:, cols] + rbuf[s]

        finish(z)
        for d in (1, 2, 3):
            @pl.when(z - d >= 0)
            def _():
                finish(z - d)

            @pl.when(z + d <= 3)
            def _():
                finish(z + d)

    for r in range(4):
        for kc in range(r + 1):
            @pl.when((r <= z) & (z < 3))
            def _():
                t_up(r, kc).wait_send()

            @pl.when((r >= z) & (z > 0))
            def _():
                t_dn(r, kc).wait_send()

            t_xn(r, kc).wait_send()
            t_sib(r, kc).wait_send()
            t_fwd(r, kc).wait_send()
        for s in range(4):
            @pl.when((s <= z) & (z < 3))
            def _():
                pz(s, r, True).wait_send()

            @pl.when((s >= z) & (z > 0))
            def _():
                pz(s, r, False).wait_send()

        px(0, c, r).wait_send()
        px(1, c, r).wait_send()
        px(2, xn, r).wait_send()
        if G == 2:
            rs(r).wait_send()


def body(G, factor, pivots, constraints):
    nb, piece, order_m = factor.shape
    strip = constraints.shape[2]
    assert strip == W and order_m == 4 * W and piece * 4 == W
    first = (lax.axis_index("row") * 4 + lax.axis_index("col")) * piece
    row_ids = first + lax.broadcasted_iota(jnp.int32, factor.shape, 1)
    col_ids = lax.broadcasted_iota(jnp.int32, factor.shape, 2)
    tri = jnp.where(col_ids < row_ids, factor, jnp.where(col_ids == row_ids, pivots[:, :, None], 0.0))
    tin = tri.reshape(nb, piece, 4, W).transpose(2, 0, 1, 3)
    rows_out = 2 * W if G == 2 else 4 * W
    dma = pltpu.SemaphoreType.DMA
    half = (4, 2 * W, W) if G == 2 else (1, 8, 128)
    result = pl.pallas_call(
        functools.partial(kernel, G, nb),
        out_shape=jax.ShapeDtypeStruct((rows_out, 4 * W), f32),
        in_specs=[pl.BlockSpec(memory_space=pltpu.VMEM), pl.BlockSpec(memory_space=pl.ANY)],
        out_specs=pl.BlockSpec(memory_space=pltpu.VMEM),
        scratch_shapes=[
            pltpu.VMEM((4, nb, 4 * W, W), f32),
            pltpu.VMEM((nb, 4 * W, W), f32),
            pltpu.VMEM((nb, 4 * W, W), bf16),
            pltpu.VMEM((nb, 4 * W, W), bf16),
            pltpu.VMEM((W, W), f32),
            pltpu.VMEM((4, 4, nb * W, W), bf16),
            pltpu.VMEM((4, 4, W, nb * W), bf16),
            pltpu.VMEM(half, f32),
            pltpu.VMEM(half, f32),
            dma,
            dma((5, 4, 4)),
            dma((4, 4, 4)),
            dma((2, 4, 4)),
            dma((4, 4)),
            dma((3, 4)),
            dma((3, 4)),
            dma((4,)),
            dma((4,)),
        ],
        compiler_params=pltpu.CompilerParams(
            collective_id=0, has_side_effects=True, vmem_limit_bytes=52 << 20),
    )(tin, constraints)
    if G != 2:
        result = lax.psum_scatter(result, "grp", scatter_dimension=0, tiled=True)
    return result[None]


def solution(mesh):
    in_specs = (
        P("grp", ("row", "col"), None),
        P("grp", ("row", "col")),
        P("grp", None, ("col", "row")),
    )
    return jax.shard_map(
        functools.partial(body, mesh.shape["grp"]), mesh=mesh, in_specs=in_specs,
        out_specs=P("row", "grp", "col"), check_vma=False)
```

time: 285 us -> 125 us (0.44)
  waiting for transfers between devices: 225 us -> 0 us
  Pallas kernels: 0 us -> 121 us
  blocking collectives: 23.4 us -> 0 us
  matrix products: 22.5 us -> 0 us
  between operations: 13.1 us -> 0.03 us
  local copies, waits for them, and re-layouts: 0.08 us -> 3.2 us
    all_gather x3 -> x0, waiting for transfers between devices: 171 us -> none  [the longest x1 82.2 us: body(): column_panel = lax.all_gather(projected, 'row', axis=2, tiled=True)]
    pallas_call x0 -> x1, Pallas kernels: none -> 121 us  [body(): pl.pallas_call(functools.partial(kernel, G, nb), out_shape=jax.ShapeDtype...]
    reduce_scatter x1 -> x0, waiting for transfers between devices: 52.7 us -> none  [body(): summed = lax.psum_scatter(gram_tile, 'grp', scatter_dimension=0, tiled=True)]
    all_gather x1 -> x0, blocking collectives: 23.4 us -> none  [body(): pivot_piece = lax.all_gather(pivots, ('row', 'col'), axis=1, tiled=True)]
    dot_general x2 -> x0, matrix products: 22.5 us -> none  [the longest x1 12.5 us: body(): jnp.einsum('brm,bms->brs', triangle, constraints, precision=exact_mode, p...]
    unnamed x1, local copies, waits for them, and re-layouts: 0.08 us -> 3.16 us
  transfers between devices with their start and end apart: 4 -> 0, of which waited for: 4 -> 0; matrix products, arithmetic and copies ran while one was open for 0% -> 0% of each run, Pallas kernels for 0% -> 0%
where the time goes in v1:
time: 125 us
  Pallas kernels  121 us (97%)
  local copies, waits for them, and re-layouts  3.2 us (3%)
    pallas_call x1, Pallas kernels, body(): pl.pallas_call(functools.partial(kernel, G, nb), out_shape=jax.ShapeDtype...  121 us
    unnamed x1, local copies, waits for them, and re-layouts  3.16 us

profile of v1, /device:TPU:0, one launch (start us, length us, event | category | flops | bytes accessed | tf_op | source)
XLA Modules:
  0.0 125.3 jit_solution(3085690127969202450)
XLA Ops:
  0.0 1.2 select_select_fusion
  1.2 120.9 %shard_map.37 = f32[512,1024]{1,0:T(8,128)} custom-call(f32[4,2,64,256]{3,2,1,0:T(8,128)S(1)} %bitcast.8, f32[2,1024,256]{2,1,0:T(8,128)} %c_hbm.1), custom_call_target="tpu_custom_call" | custom-call | tf_op jit(solution)/shard_map/pallas_call | solution.py:298
  122.2 3.2 %copy.9 = f32[1,512,1024]{2,1,0:T(8,128)} copy(f32[1,512,1024]{2,1,0:T(8,128)} %bitcast.9) | data formatting | bytes 4194304
  (2 shorter events, 0.0 us)

commit v2 on v1

--- a/solution.py
+++ b/solution.py
@@ -12,15 +12,15 @@
 W = 256
 
 
-def kernel(G, nb, tin, c_hbm, out, tbuf, cbuf, chi, clo, acc, colbuf, rowt, sbuf, rbuf,
-           csem, tss, trs, pzs, pzr, pxs, pxr, rss, rsr):
+def kernel(G, nb, fac, piv, c_hbm, out, tbuf, cbuf, chi, clo, acc, colbuf, rowt, obuf, sbuf, rbuf,
+           csem, tss, trs, pzs, pzr, phs, phr, pxs, pxr, rss, rsr, osem):
     g, z, c = lax.axis_index("grp"), lax.axis_index("row"), lax.axis_index("col")
     sib = c + 1 - 2 * (c % 2)
     xn = (c + 2) % 4
     d_up, d_dn = (g, z + 1, c), (g, z - 1, c)
     d_xn, d_sib = (g, z, xn), (g, z, sib)
     d_y = (1 - g, z, c)
-    piece = tin.shape[2]
+    piece = fac.shape[1]
 
     def order(zz, j):
         if j == 0:
@@ -55,7 +55,13 @@
     for kc in range(4):
         @pl.when(kc <= z)
         def _():
-            tbuf[kc, :, pl.ds(pl.multiple_of(W * z + piece * c, piece), piece), :] = tin[kc]
+            start = W * z + piece * c
+            rows = start + lax.broadcasted_iota(jnp.int32, (piece, W), 0)
+            cols = W * kc + lax.broadcasted_iota(jnp.int32, (piece, W), 1)
+            for b in range(nb):
+                diag = jnp.where(cols == rows, jnp.broadcast_to(piv[b:b + 1, :], (piece, W)), 0.0)
+                tbuf[kc, b, pl.ds(pl.multiple_of(start, piece), piece), :] = jnp.where(
+                    cols < rows, fac[b, :, W * kc:W * (kc + 1)], diag)
 
     pl.semaphore_wait(bar, (3 if G == 2 else 2) + (z + 3) // 4 + 1 - z // 3)
 
@@ -160,43 +166,70 @@
         hi = cc.astype(bf16)
         chi[b] = hi
         clo[b] = (cc - hi.astype(f32)).astype(bf16)
-    for j in range(1, 4):
-        t_first(j)
-        t_second(j - 1)
-        project(j - 1)
+    t_first(1)
+    t_first(2)
+    t_second(0)
+    project(0)
+    t_second(1)
+    project(1)
+    t_first(3)
+    t_second(2)
+    project(2)
     t_second(3)
     project(3)
 
-    def block(cp, s):
-        total = jnp.dot(rowt[cp, 0], colbuf[s, 0], preferred_element_type=f32)
+    H = W // 2
+
+    def block(cp, s, lo, n):
+        total = jnp.dot(rowt[cp, 0], colbuf[s, 0, :, lo:lo + n], preferred_element_type=f32)
         for rg in range(1, 4):
-            total += jnp.dot(rowt[cp, rg], colbuf[s, rg], preferred_element_type=f32)
+            total += jnp.dot(rowt[cp, rg], colbuf[s, rg, :, lo:lo + n], preferred_element_type=f32)
         return total
 
-    def rs(s):
+    def rs(s, h):
         return pltpu.make_async_remote_copy(
-            src_ref=sbuf.at[s], dst_ref=rbuf.at[s], send_sem=rss.at[s], recv_sem=rsr.at[s],
+            src_ref=sbuf.at[s, h], dst_ref=rbuf.at[s, h], send_sem=rss.at[s, h], recv_sem=rsr.at[s, h],
             device_id=d_y, device_id_type=MESH)
 
-    def gram(s):
-        cols = pl.ds(pl.multiple_of(W * s, W), W)
+    def emit(s, h):
+        cols = pl.ds(pl.multiple_of(W * s + H * h, H), H)
+        return pltpu.make_async_copy(obuf.at[:, cols], out.at[:, cols], osem.at[s, h])
+
+    def gram(s, halves):
+        lo, n = H * halves[0], H * len(halves)
+        cols = pl.ds(pl.multiple_of(W * s + lo, H), n)
         if G == 2:
             @pl.loop(0, 2)
             def _(i):
-                sbuf[s, pl.ds(pl.multiple_of(W * i, W), W), :] = block(2 * (1 - g) + i, s)
-
-            rs(s).start()
+                rows = pl.ds(pl.multiple_of(W * i, W), W)
+                t = block(2 * (1 - g) + i, s, lo, n)
+                for k, h in enumerate(halves):
+                    sbuf[s, h, rows, :] = t[:, H * k:H * (k + 1)]
+
+            for h in halves:
+                rs(s, h).start()
 
             @pl.loop(0, 2)
             def _(i):
-                out[pl.ds(pl.multiple_of(W * i, W), W), cols] = block(2 * g + i, s)
+                obuf[pl.ds(pl.multiple_of(W * i, W), W), cols] = block(2 * g + i, s, lo, n)
         else:
             @pl.loop(0, 4)
             def _(i):
-                out[pl.ds(pl.multiple_of(W * i, W), W), cols] = block(i, s)
-
-    def z_arrivals(d, i):
-        lo, hi = z - d, z + d
+                obuf[pl.ds(pl.multiple_of(W * i, W), W), cols] = block(i, s, lo, n)
+
+    def finish(s):
+        for h in (0, 1):
+            if G == 2:
+                cols = pl.ds(pl.multiple_of(W * s + H * h, H), H)
+                rs(s, h).wait_recv()
+                obuf[:, cols] = obuf[:, cols] + rbuf[s, h]
+            emit(s, h).start()
+
+    def ph(s, rg, h, up):
+        return remote(colbuf.at[s, rg, :, H * h:H * (h + 1)], phs.at[rg, h], phr.at[rg, h], d_up if up else d_dn)
+
+    def near(i):
+        lo, hi = z - 1, z + 1
 
         @pl.when(lo >= 0)
         def _():
@@ -216,43 +249,49 @@
             def _():
                 pz(hi, rg, False).start()
 
+    def second(s, up):
+        for i in range(4):
+            pz(s, order(s, i), up).wait_recv()
+
+        @pl.when((z == 1) | (z == 2))
+        def _():
+            for h in (0, 1):
+                for rg in range(4):
+                    ph(s, rg, h, up).start()
+
+        gram(s, (0, 1))
+
+    def third(s, up):
+        for h in (0, 1):
+            for rg in range(4):
+                ph(s, rg, h, up).wait_recv()
+            gram(s, (h,))
+
+    def each(d, fn):
+        @pl.when(z - d >= 0)
+        def _():
+            fn(z - d, True)
+
+        @pl.when(z + d <= 3)
+        def _():
+            fn(z + d, False)
+
     for i in range(4):
+        near(i)
         r = order(z, i)
         px(0, c, r).wait_recv()
         px(2, xn, r).start()
-        z_arrivals(1, i)
     for i in range(4):
         px(1, c, i).wait_recv()
         px(2, c, i).wait_recv()
-    gram(z)
-    for d in (1, 2, 3):
-        if d > 1:
-            for i in range(4):
-                z_arrivals(d, i)
-
-        @pl.when(z - d >= 0)
-        def _():
-            gram(z - d)
-
-        @pl.when(z + d <= 3)
-        def _():
-            gram(z + d)
-
-    if G == 2:
-        def finish(s):
-            cols = pl.ds(pl.multiple_of(W * s, W), W)
-            rs(s).wait_recv()
-            out[:, cols] = out[:, cols] + rbuf[s]
-
-        finish(z)
-        for d in (1, 2, 3):
-            @pl.when(z - d >= 0)
-            def _():
-                finish(z - d)
-
-            @pl.when(z + d <= 3)
-            def _():
-                finish(z + d)
+    gram(z, (0, 1))
+    each(1, lambda s, up: gram(s, (0, 1)))
+    each(2, second)
+    finish(z)
+    each(1, lambda s, up: finish(s))
+    each(2, lambda s, up: finish(s))
+    each(3, third)
+    each(3, lambda s, up: finish(s))
 
     for r in range(4):
         for kc in range(r + 1):
@@ -268,38 +307,43 @@
             t_sib(r, kc).wait_send()
             t_fwd(r, kc).wait_send()
         for s in range(4):
-            @pl.when((s <= z) & (z < 3))
+            @pl.when((s <= z) & (z < 3) & (z - s < 2))
             def _():
                 pz(s, r, True).wait_send()
 
-            @pl.when((s >= z) & (z > 0))
+            @pl.when((s >= z) & (z > 0) & (s - z < 2))
             def _():
                 pz(s, r, False).wait_send()
 
         px(0, c, r).wait_send()
         px(1, c, r).wait_send()
         px(2, xn, r).wait_send()
-        if G == 2:
-            rs(r).wait_send()
+        for h in (0, 1):
+            @pl.when((z == 1) | (z == 2))
+            def _():
+                ph(3, r, h, False).wait_send()
+
+            if G == 2:
+                rs(r, h).wait_send()
+            emit(r, h).wait()
 
 
 def body(G, factor, pivots, constraints):
     nb, piece, order_m = factor.shape
     strip = constraints.shape[2]
     assert strip == W and order_m == 4 * W and piece * 4 == W
-    first = (lax.axis_index("row") * 4 + lax.axis_index("col")) * piece
-    row_ids = first + lax.broadcasted_iota(jnp.int32, factor.shape, 1)
-    col_ids = lax.broadcasted_iota(jnp.int32, factor.shape, 2)
-    tri = jnp.where(col_ids < row_ids, factor, jnp.where(col_ids == row_ids, pivots[:, :, None], 0.0))
-    tin = tri.reshape(nb, piece, 4, W).transpose(2, 0, 1, 3)
     rows_out = 2 * W if G == 2 else 4 * W
     dma = pltpu.SemaphoreType.DMA
-    half = (4, 2 * W, W) if G == 2 else (1, 8, 128)
+    half = (4, 2, 2 * W, W // 2) if G == 2 else (1, 1, 8, 128)
     result = pl.pallas_call(
         functools.partial(kernel, G, nb),
         out_shape=jax.ShapeDtypeStruct((rows_out, 4 * W), f32),
-        in_specs=[pl.BlockSpec(memory_space=pltpu.VMEM), pl.BlockSpec(memory_space=pl.ANY)],
-        out_specs=pl.BlockSpec(memory_space=pltpu.VMEM),
+        in_specs=[
+            pl.BlockSpec(memory_space=pltpu.VMEM),
+            pl.BlockSpec(memory_space=pltpu.VMEM),
+            pl.BlockSpec(memory_space=pl.ANY),
+        ],
+        out_specs=pl.BlockSpec(memory_space=pl.ANY),
         scratch_shapes=[
             pltpu.VMEM((4, nb, 4 * W, W), f32),
             pltpu.VMEM((nb, 4 * W, W), f32),
@@ -308,6 +352,7 @@
             pltpu.VMEM((W, W), f32),
             pltpu.VMEM((4, 4, nb * W, W), bf16),
             pltpu.VMEM((4, 4, W, nb * W), bf16),
+            pltpu.VMEM((rows_out, 4 * W), f32),
             pltpu.VMEM(half, f32),
             pltpu.VMEM(half, f32),
             dma,
@@ -315,14 +360,17 @@
             dma((4, 4, 4)),
             dma((2, 4, 4)),
             dma((4, 4)),
+            dma((4, 2)),
+            dma((4, 2)),
             dma((3, 4)),
             dma((3, 4)),
-            dma((4,)),
-            dma((4,)),
+            dma((4, 2)),
+            dma((4, 2)),
+            dma((4, 2)),
         ],
         compiler_params=pltpu.CompilerParams(
             collective_id=0, has_side_effects=True, vmem_limit_bytes=52 << 20),
-    )(tin, constraints)
+    )(factor, jnp.tile(pivots, (1, 4)), constraints)
     if G != 2:
         result = lax.psum_scatter(result, "grp", scatter_dimension=0, tiled=True)
     return result[None]

time: 125 us -> 120 us (0.960)
  Pallas kernels: 121 us -> 114 us
  local copies, waits for them, and re-layouts: 3.2 us -> 4.96 us
    pallas_call x1, Pallas kernels: 121 us -> 114 us  [body(): pl.pallas_call(functools.partial(kernel, G, nb), out_shape=jax.ShapeDtype...]
    unnamed x1 -> x3, local copies, waits for them, and re-layouts: 3.16 us -> 4.2 us
where the time goes in v2:
time: 120 us; the launch traced here: 119 us
  Pallas kernels  114 us (95%)
  local copies, waits for them, and re-layouts  4.96 us (4%)
    pallas_call x1, Pallas kernels, body(): pl.pallas_call(functools.partial(kernel, G, nb), out_shape=jax.ShapeDtype...  114 us
    unnamed x3, local copies, waits for them, and re-layouts  4.2 us

profile of v2, /device:TPU:0, one launch (start us, length us, event | category | flops | bytes accessed | tf_op | source)
XLA Modules:
  0.0 119.3 jit_solution(3131079715643375639)
XLA Ops:
  0.0 0.7 tile.4
  0.7 0.1 tile.10.piv
  0.8 0.0 copy-start
  0.8 1.0 copy-done
  1.8 114.4 %shard_map.37 = f32[512,1024]{1,0:T(8,128)} custom-call(f32[2,64,1024]{2,1,0:T(8,128)S(1)} %copy-done, f32[2,256]{1,0:T(2,128)S(1)} %tile.10.piv, f32[2,1024,256]{2,1,0:T(8,128)} %c_hbm.1), custom_call_target="tpu_custom_call" | custom-call | tf_op jit(solution)/shard_map/pallas_call | solution.py:338
  116.2 3.2 %copy.5 = f32[1,512,1024]{2,1,0:T(8,128)} copy(f32[1,512,1024]{2,1,0:T(8,128)} %bitcast.1) | data formatting | bytes 4194304
Async XLA Ops:
  0.8 1.0 copy-start

commit v3 on v2

--- a/solution.py
+++ b/solution.py
@@ -170,9 +170,9 @@
     t_first(2)
     t_second(0)
     project(0)
+    t_first(3)
     t_second(1)
     project(1)
-    t_first(3)
     t_second(2)
     project(2)
     t_second(3)
@@ -289,8 +289,8 @@
     each(2, second)
     finish(z)
     each(1, lambda s, up: finish(s))
+    each(3, third)
     each(2, lambda s, up: finish(s))
-    each(3, third)
     each(3, lambda s, up: finish(s))
 
     for r in range(4):

time: 120 us -> 115 us (0.958)
  Pallas kernels: 114 us -> 110 us
    pallas_call x1, Pallas kernels: 114 us -> 110 us  [body(): pl.pallas_call(functools.partial(kernel, G, nb), out_shape=jax.ShapeDtype...]
where the time goes in v3:
time: 115 us
  Pallas kernels  110 us (96%)
  local copies, waits for them, and re-layouts  4.96 us (4%)
    pallas_call x1, Pallas kernels, body(): pl.pallas_call(functools.partial(kernel, G, nb), out_shape=jax.ShapeDtype...  110 us
    unnamed x3, local copies, waits for them, and re-layouts  4.2 us

profile of v3, /device:TPU:0, one launch (start us, length us, event | category | flops | bytes accessed | tf_op | source)
XLA Modules:
  0.0 114.6 jit_solution(15595723291891515584)
XLA Ops:
  0.0 0.7 tile.4
  0.7 0.1 tile.10.piv
  0.8 0.0 copy-start
  0.8 1.0 copy-done
  1.8 109.6 %shard_map.37 = f32[512,1024]{1,0:T(8,128)} custom-call(f32[2,64,1024]{2,1,0:T(8,128)S(1)} %copy-done, f32[2,256]{1,0:T(2,128)S(1)} %tile.10.piv, f32[2,1024,256]{2,1,0:T(8,128)} %c_hbm.1), custom_call_target="tpu_custom_call" | custom-call | tf_op jit(solution)/shard_map/pallas_call | solution.py:338
  111.4 3.2 %copy.5 = f32[1,512,1024]{2,1,0:T(8,128)} copy(f32[1,512,1024]{2,1,0:T(8,128)} %bitcast.1) | data formatting | bytes 4194304
Async XLA Ops:
  0.8 1.0 copy-start
